TPU v7x, 128 devices: a whole 4x4x4 slice. The times are simulated.
128 devices in a mesh: date: 8 (over y, core), strip: 16 (over z, x).
Axes of the slice: x: 4, y: 4, z: 4, core: 2. Of those that a mesh axis runs over, the one named last changes fastest.
Arguments:
- stack: float32 [64, 1024, 2048], P('date', 'strip'), may hold values from -6 to 6
- spatial_taps: float32 [13], replicated, may hold values from 0.2 to 1
- temporal_taps: float32 [2, 5], replicated, may hold values from -0.25 to 0.25
- foot_tile: int32 [16384], P(('date', 'strip')), may hold values from 0 to 1
- foot_row: int32 [16384], P(('date', 'strip')), may hold values from 0 to 63
- foot_count: int32 [16384], P(('date', 'strip')), may hold values from 1 to 128
- foot_owner: int32 [16384, 1], P(('date', 'strip')), may hold values from 0 to 127; in each aligned block of 128 rows (0 to 127, 128 to 255, ...) at most 2 rows name the same one
Outputs:
- residual: float32 [64, 1024, 2048], P(None, 'strip', 'date')
- anomaly: float32 [128, 256, 64], P(('date', 'strip'))
- asset_series: float32 [128, 64], P(('date', 'strip'))
Inputs may be any that keep to these rules, and one draw needn't show every extreme that they name: `foot_owner`: among the footprints of one block, no owner appears more than 2 times, a bound that some block reaches; every owner has some footprint.
All inputs are finite; a program needn't handle non-finite values.
Results may differ from a plain program's by a relative error of at most 0.000075.
Values sent between devices are 32-bit elements; how exact they have to be, the bound alone decides.
A program may use at most 128 MiB of HBM per device.

v0:
```python
import jax
import jax.numpy as jnp
from jax import lax
from jax.sharding import PartitionSpec as P

TILE = 128
RADIUS = 6
REACH = 2
DILATION = 8
PAIR_CAP = 2


def with_halo(value, sides, width):
    for axis, dim in sides:
        peers, length = (lax.axis_size(axis), value.shape[dim])
        up = [(i, (i + 1) % peers) for i in range(peers - 1)]
        down = [(j, i) for i, j in up]
        last = lax.slice_in_dim(value, length - width, length, axis=dim)
        initial = lax.slice_in_dim(value, 0, width, axis=dim)
        before = lax.ppermute(last, axis, up)
        after = lax.ppermute(initial, axis, down)
        value = jnp.concatenate([before, value, after], axis=dim)
    return value


def taps_pass(padded, weights, axis_num, length):
    summed = weights[0] * lax.slice_in_dim(padded, 0, length, axis=axis_num)
    for k in range(1, weights.shape[0]):
        summed = summed + weights[k] * lax.slice_in_dim(padded, k, k + length, axis=axis_num)
    return summed


def temporal_filter(series, temporal_taps):
    date_count = series.shape[0]
    for level_idx, spacing in enumerate((1, DILATION)):
        margin = REACH * spacing
        padded = jnp.pad(series, ((margin, margin), (0, 0), (0, 0)))
        smooth_part = temporal_taps[level_idx, 0] * lax.slice_in_dim(padded, 0, date_count, axis=0)
        for k in range(1, 2 * REACH + 1):
            smooth_part = smooth_part + temporal_taps[level_idx, k] * lax.slice_in_dim(
                padded, k * spacing, k * spacing + date_count, axis=0
            )
        series = series - smooth_part
    return series


def shards(stack, spatial_taps, temporal_taps, foot_tile, foot_row, foot_count, foot_owner):
    weights = spatial_taps / jnp.sum(spatial_taps)
    padded = jnp.pad(stack, ((0, 0), (0, 0), (RADIUS, RADIUS)))
    across = taps_pass(padded, weights, 2, stack.shape[2])
    rimmed = with_halo(across, (("strip", 1),), RADIUS)
    corrected = stack - taps_pass(rimmed, weights, 1, stack.shape[1])
    residual = temporal_filter(
        lax.all_to_all(corrected, "date", split_axis=2, concat_axis=0, tiled=True), temporal_taps
    )
    date_count, row_count, col_count = residual.shape
    tile_view = residual.reshape(date_count, row_count, col_count // TILE, TILE)
    picked = tile_view[:, foot_row, foot_tile, :]
    counts = foot_count.astype(jnp.float32)
    inside = (jnp.arange(TILE, dtype=jnp.int32)[None, :] < foot_count[:, None]).astype(jnp.float32)
    foot_mean = jnp.sum(picked * inside[None], axis=2) / counts[None, :]
    owners = foot_owner[:, 0]
    position = jnp.arange(owners.shape[0], dtype=jnp.int32)
    earlier = (owners[:, None] == owners[None, :]) & (position[None, :] < position[:, None])
    slot_rank = jnp.sum(earlier.astype(jnp.int32), axis=1)
    date_devices = lax.axis_size("date")
    strip_devices = lax.axis_size("strip")
    devices_all = date_devices * strip_devices
    dest_slot = owners * PAIR_CAP + slot_rank
    onehot = (
        dest_slot[:, None] == jnp.arange(devices_all * PAIR_CAP, dtype=jnp.int32)[None, :]
    ).astype(jnp.float32)
    outgoing = jnp.einsum("fk,tf->kt", onehot, foot_mean, precision=lax.Precision.HIGHEST)
    out_weight = jnp.einsum("fk,f->k", onehot, counts, precision=lax.Precision.HIGHEST)
    received, weight_in = (
        lax.all_to_all(
            outgoing.reshape(devices_all, PAIR_CAP, date_count),
            ("date", "strip"),
            split_axis=0,
            concat_axis=0,
            tiled=True,
        ),
        lax.all_to_all(
            out_weight.reshape(devices_all, PAIR_CAP),
            ("date", "strip"),
            split_axis=0,
            concat_axis=0,
            tiled=True,
        ),
    )
    total_weight = jnp.sum(weight_in)
    asset_mean = jnp.sum(weight_in[:, :, None] * received, axis=(0, 1)) / total_weight
    anomaly = jnp.where(weight_in[:, :, None] > 0, received - asset_mean[None, None, :], 0.0)
    return (residual, anomaly.reshape(1, devices_all * PAIR_CAP, date_count), asset_mean[None, :])


def solution(mesh):
    placed = (
        P("date", "strip", None),
        P(),
        P(),
        P(("date", "strip")),
        P(("date", "strip")),
        P(("date", "strip")),
        P(("date", "strip"), None),
    )
    return jax.shard_map(
        shards,
        mesh=mesh,
        in_specs=placed,
        out_specs=(
            P(None, "strip", "date"),
            P(("date", "strip"), None, None),
            P(("date", "strip"), None),
        ),
        check_vma=False,
    )
```

profile of v0, /device:TPU:1, one launch (start us, length us, event | category | flops | bytes accessed | tf_op | source)
XLA Modules:
  0.0 279.2 jit_solution(2231093077993058063)
XLA Ops:
  0.6 1.3 reduce_sum.47
  1.9 1.3 broadcast_divide_fusion.1
  3.2 0.7 fusion.75
  3.9 6.6 %copy.37 = f32[8,64,2048]{2,0,1:T(8,128)} copy(f32[8,64,2048]{2,1,0:T(8,128)} %param.7) | data formatting | bytes 8388608 | tf_op args[0]
  10.5 42.0 %multiply_add_fusion = f32[8,64,2048]{2,0,1:T(8,128)} fusion(f32[8,64,2048]{2,0,1:T(8,128)} %copy.37, f32[]{:T(128)} %bitcast.12, f32[]{:T(128)} %bitcast.11, f32[]{:T(128)} %bitcast.10, f32[]{:T(128)} %bitcast.9, f32[]{:T(128)} %bitcast.8, f32[]{:T(128)} %bitcast.7, f32[]{:T(128)} %bitcast.6, f32[]{:T(128)} %bitcast.5, f32[]{:T(128)} %bitcast.4, ...), kind=kLoop, calls=%fused_computation.79 | loop fusion | flops 26214400 | bytes 8388660 | tf_op jit(solution)/shard_map/add | solution.py:29
  52.6 1.2 fusion.73
  53.7 4.0 %collective-permute-start = (f32[8,6,2048]{2,0,1:T(8,128)S(1)}, f32[8,6,2048]{2,0,1:T(8,128)S(1)}, u32[]{:S(2)}, u32[]{:S(2)}) collective-permute-start(f32[8,6,2048]{2,0,1:T(8,128)S(1)} %get-tuple-element.18), channel_id=1, source_target_pairs={{0,1},{1,2},{2,3},{3,4},{4,5},{5,6},{6,7},{7,8},{8,9},{9,10},{10,1... | collective-permute-start | bytes 1179656 | tf_op jit(solution)/shard_map/ppermute | solution.py:20
  57.7 1.5 collective-permute-start.1
  59.2 6.3 %collective-permute-done = f32[8,6,2048]{2,0,1:T(8,128)S(1)} collective-permute-done((f32[8,6,2048]{2,0,1:T(8,128)S(1)}, f32[8,6,2048]{2,0,1:T(8,128)S(1)}, u32[]{:S(2)}, u32[]{:S(2)}) %collective-permute-start) | collective-permute-done | bytes 393248 | tf_op jit(solution)/shard_map/ppermute | solution.py:20
  65.5 3.8 %collective-permute-done.1 = f32[8,6,2048]{2,0,1:T(8,128)S(1)} collective-permute-done((f32[8,6,2048]{2,0,1:T(8,128)S(1)}, f32[8,6,2048]{2,0,1:T(8,128)S(1)}, u32[]{:S(2)}, u32[]{:S(2)}) %collective-permute-start.1) | collective-permute-done | bytes 393248 | tf_op jit(solution)/shard_map/ppermute | solution.py:21
  69.3 32.9 %fusion.4 = f32[8,64,2048]{2,0,1:T(8,128)} fusion(f32[8,64,2048]{2,0,1:T(8,128)} %multiply_add_fusion, f32[8,6,2048]{2,0,1:T(8,128)S(1)} %collective-permute-done.1, f32[8,6,2048]{2,0,1:T(8,128)S(1)} %collective-permute-done, f32[]{:T(128)} %bitcast.12, f32[]{:T(128)} %bitcast.11, f32[]{:T(128)} %bitcast.10, f32[]{:T(128)} %bitcast.9, f32[]{:T(128)} %bitcast.8, ...), kind=kLoop, calls=%fused_computation.29 | loop fusion | flops 39845888 | bytes 13369396 | tf_op jit(solution)/shard_map/sub | solution.py:52
  102.1 7.5 %copy.38 = f32[8,64,2048]{1,0,2:T(8,128)} copy(f32[8,64,2048]{2,0,1:T(8,128)} %fusion.4) | data formatting | bytes 8388608 | tf_op jit(solution)/shard_map/sub | solution.py:52
  109.6 9.8 %reshape.84 = f32[8,1,131072]{2,1,0:T(1,128)} reshape(f32[2048,8,64]{2,1,0:T(8,128)} %bitcast.46) | data formatting | bytes 8388608
  119.4 0.0 copy-start.1
  119.4 0.0 copy-start.2
  119.4 0.0 copy-start
  119.4 0.0 copy-start.3
  119.4 0.0 copy-start.4
  119.5 6.5 %all-to-all-start = ((f32[8,1,131072]{2,1,0:T(1,128)}), f32[8,1,131072]{2,1,0:T(1,128)}, u32[]{:S(2)}, u32[]{:S(2)}) async-start(f32[8,1,131072]{2,1,0:T(1,128)} %reshape.84), calls=%async_computation | async-start | bytes 8388608 | tf_op jit(solution)/shard_map/all_to_all | solution.py:54
  125.9 0.0 copy-done.1
  125.9 0.0 copy-done.2
  125.9 0.2 convert_reduce_fusion
  126.1 0.2 fusion.58
  126.3 0.8 all_to_all.28
  127.1 0.0 copy-done
  127.1 0.7 fusion.74
  127.8 0.0 copy-done.3
  127.8 0.0 copy-done.4
  127.8 0.1 fusion.63
  127.9 46.9 %all-to-all-done = f32[8,1,131072]{2,1,0:T(1,128)} async-done(((f32[8,1,131072]{2,1,0:T(1,128)}), f32[8,1,131072]{2,1,0:T(1,128)}, u32[]{:S(2)}, u32[]{:S(2)}) %all-to-all-start) | async-done | bytes 4194336 | tf_op jit(solution)/shard_map/all_to_all | solution.py:54
  174.8 10.6 %all-to-all-start.1 = ((f32[128,1,2]{2,1,0:T(1,128)}), f32[128,1,2]{2,1,0:T(1,128)S(1)}, u32[]{:S(2)}, u32[]{:S(2)}) async-start(f32[128,1,2]{2,1,0:T(1,128)} %bitcast.31), calls=%async_computation.1 | async-start | bytes 131072 | tf_op jit(solution)/shard_map/all_to_all | solution.py:83
  185.4 0.5 broadcast.84
  185.9 13.8 %reduce.3 = f32[8,131072]{1,0:T(8,128)} reduce(f32[8,1,131072]{2,1,0:T(1,128)} %all-to-all-done, f32[]{:T(128)} %broadcast.84), dimensions={1}, to_apply=%all_to_all.24.reduce_sub_computation | reduce | bytes 8388612 | tf_op jit(solution)/shard_map/all_to_all | solution.py:54
  199.7 8.7 %reshape.85 = f32[2048,8,64]{2,1,0:T(8,128)} reshape(f32[8,131072]{1,0:T(8,128)} %reduce.3) | data formatting | bytes 8388608
  208.4 6.8 %copy.39 = f32[8,8,64,256]{3,2,1,0:T(8,128)} copy(f32[8,8,64,256]{2,1,3,0:T(8,128)} %bitcast.47) | data formatting | bytes 8388608 | tf_op jit(solution)/shard_map/all_to_all | solution.py:54
  215.1 12.2 %add_subtract_fusion = f32[64,64,256]{2,1,0:T(8,128)S(1)} fusion(f32[64,64,256]{2,1,0:T(8,128)} %bitcast.48, f32[]{:T(128)} %bitcast.20, f32[]{:T(128)} %bitcast.19, f32[]{:T(128)} %bitcast.18, f32[]{:T(128)} %bitcast.17, f32[]{:T(128)} %bitcast.16), kind=kLoop, calls=%fused_computation.72 | loop fusion | flops 10485760 | bytes 8388628 | tf_op jit(solution)/shard_map/sub | solution.py:43
  227.3 6.6 %fusion.38 = f32[64,64,256]{2,1,0:T(8,128)} fusion(f32[64,64,256]{2,1,0:T(8,128)S(1)} %add_subtract_fusion, f32[]{:T(128)} %bitcast.25, f32[]{:T(128)} %bitcast.24, f32[]{:T(128)} %bitcast.23, f32[]{:T(128)} %bitcast.22, f32[]{:T(128)} %bitcast.21), kind=kLoop, calls=%fused_computation.63 | loop fusion | flops 10485760 | bytes 8388628 | tf_op jit(solution)/shard_map/sub | solution.py:43
  233.9 5.8 %reshape.61 = f32[64,64,2,128]{3,2,1,0:T(2,128)} reshape(f32[64,64,256]{2,1,0:T(8,128)} %fusion.38) | data formatting | bytes 8388608 | tf_op jit(solution)/shard_map/reshape | solution.py:57
  239.7 6.5 %copy.41 = f32[64,64,2,128]{3,0,2,1:T(8,128)} copy(f32[64,64,2,128]{3,2,1,0:T(2,128)} %reshape.61) | data formatting | bytes 8388608 | tf_op jit(solution)/shard_map/reshape | solution.py:57
  246.2 5.0 %gather_fusion = f32[128,64,128]{2,1,0:T(8,128)} fusion(f32[64,64,2,128]{3,0,2,1:T(8,128)} %copy.41, s32[128]{0:T(128)S(1)} %fusion.67), kind=kCustom, calls=%fused_computation | custom fusion | bytes 8389632 | tf_op jit(solution)/shard_map/gather | solution.py:58
  251.3 3.4 %multiply_reduce_fusion = f32[128,64]{1,0:T(8,128)S(1)} fusion(f32[128,64,128]{2,1,0:T(8,128)} %gather_fusion, f32[128,128]{1,0:T(8,128)S(1)} %fusion.63), kind=kLoop, calls=%fused_computation.71 | loop fusion | flops 2088960 | bytes 4292608 | tf_op jit(solution)/shard_map/reduce_sum | solution.py:61
  254.6 0.4 fusion.57
  255.0 0.8 reshape.86
  255.8 0.0 all-to-all-done.1
  255.8 9.8 %all-to-all-start.2 = ((f32[128,1,128]{2,1,0:T(1,128)}), f32[128,1,128]{2,1,0:T(1,128)S(1)}, u32[]{:S(2)}, u32[]{:S(2)}) async-start(f32[128,1,128]{2,1,0:T(1,128)} %reshape.86), calls=%async_computation.2 | async-start | bytes 131072 | tf_op jit(solution)/shard_map/all_to_all | solution.py:76
  265.6 0.8 reduce_sum.52
  266.4 8.9 %all-to-all-done.2 = f32[128,1,128]{2,1,0:T(1,128)S(1)} async-done(((f32[128,1,128]{2,1,0:T(1,128)}), f32[128,1,128]{2,1,0:T(1,128)S(1)}, u32[]{:S(2)}, u32[]{:S(2)}) %all-to-all-start.2) | async-done | bytes 65568 | tf_op jit(solution)/shard_map/all_to_all | solution.py:76
  275.2 0.8 reduce.4
  276.1 0.1 reshape.87
  276.2 0.2 multiply_reduce_fusion.1
  276.4 0.7 broadcast_divide_fusion
  277.1 1.2 fusion.76
  278.3 0.2 subtract_select_fusion
  278.5 0.7 copy.43
  (4 shorter events, 0.0 us)
Async XLA Ops:
  53.7 11.7 %collective-permute-start = (f32[8,6,2048]{2,0,1:T(8,128)S(1)}, f32[8,6,2048]{2,0,1:T(8,128)S(1)}, u32[]{:S(2)}, u32[]{:S(2)}) collective-permute-start(f32[8,6,2048]{2,0,1:T(8,128)S(1)} %get-tuple-element.18), channel_id=1, source_target_pairs={{0,1},{1,2},{2,3},{3,4},{4,5},{5,6},{6,7},{7,8},{8,9},{9,10},{10,1... | collective-permute-start | bytes 1179656 | tf_op jit(solution)/shard_map/ppermute | solution.py:20
  57.7 11.6 %collective-permute-start.1 = (f32[8,6,2048]{2,0,1:T(8,128)S(1)}, f32[8,6,2048]{2,0,1:T(8,128)S(1)}, u32[]{:S(2)}, u32[]{:S(2)}) collective-permute-start(f32[8,6,2048]{2,0,1:T(8,128)S(1)} %get-tuple-element.19), channel_id=1, source_target_pairs={{1,0},{2,1},{3,2},{4,3},{5,4},{6,5},{7,6},{8,7},{9,8},{10,9},{11,1... | collective-permute-start | bytes 1179656 | tf_op jit(solution)/shard_map/ppermute | solution.py:21
  119.4 6.5 %copy-start.1 = (s32[128]{0:T(128)S(1)}, s32[128]{0:T(128)}, u32[]{:S(2)}) copy-start(s32[128]{0:T(128)} %param.12) | copy-start | bytes 1540
  119.4 6.5 %copy-start.2 = (s32[128,1]{0,1:T(1,128)S(1)}, s32[128,1]{0,1:T(1,128)}, u32[]{:S(2)}) copy-start(s32[128,1]{0,1:T(1,128)} %param.13) | copy-start | bytes 1540
  119.4 7.7 %copy-start = (f32[2,5]{1,0:T(2,128)S(1)}, f32[2,5]{1,0:T(2,128)}, u32[]{:S(2)}) copy-start(f32[2,5]{1,0:T(2,128)} %param.9) | copy-start | bytes 124
  119.4 8.4 %copy-start.3 = (s32[128]{0:T(128)S(1)}, s32[128]{0:T(128)}, u32[]{:S(2)}) copy-start(s32[128]{0:T(128)} %param.11) | copy-start | bytes 1540
  119.4 8.4 %copy-start.4 = (s32[128]{0:T(128)S(1)}, s32[128]{0:T(128)}, u32[]{:S(2)}) copy-start(s32[128]{0:T(128)} %param.10) | copy-start | bytes 1540
  119.5 55.4 %all-to-all-start = ((f32[8,1,131072]{2,1,0:T(1,128)}), f32[8,1,131072]{2,1,0:T(1,128)}, u32[]{:S(2)}, u32[]{:S(2)}) async-start(f32[8,1,131072]{2,1,0:T(1,128)} %reshape.84), calls=%async_computation | async-start | bytes 8388608 | tf_op jit(solution)/shard_map/all_to_all | solution.py:54
  174.8 80.9 %all-to-all-start.1 = ((f32[128,1,2]{2,1,0:T(1,128)}), f32[128,1,2]{2,1,0:T(1,128)S(1)}, u32[]{:S(2)}, u32[]{:S(2)}) async-start(f32[128,1,2]{2,1,0:T(1,128)} %bitcast.31), calls=%async_computation.1 | async-start | bytes 131072 | tf_op jit(solution)/shard_map/all_to_all | solution.py:83
  255.8 19.5 %all-to-all-start.2 = ((f32[128,1,128]{2,1,0:T(1,128)}), f32[128,1,128]{2,1,0:T(1,128)S(1)}, u32[]{:S(2)}, u32[]{:S(2)}) async-start(f32[128,1,128]{2,1,0:T(1,128)} %reshape.86), calls=%async_computation.2 | async-start | bytes 131072 | tf_op jit(solution)/shard_map/all_to_all | solution.py:76
where the time goes:
time: 281 us; the launch traced here: 279 us
  other arithmetic  118 us (42%)
  waiting for transfers between devices  65.9 us (23%)
  local copies, waits for them, and re-layouts  62.2 us (22%)
  starting transfers between devices  32.2 us (11%)
    all_to_all x1, waiting for transfers between devices, shards(): lax.all_to_all(corrected, 'date', split_axis=2, concat_axis=0, tiled=True)  46.9 us
    add x1, other arithmetic, taps_pass(): summed + weights[k] * lax.slice_in_dim(padded, k, k + length, axis=axis_num)  42 us
    sub x1, other arithmetic, shards(): corrected = stack - taps_pass(rimmed, weights, 1, stack.shape[1])  32.9 us
    unnamed x16, local copies, waits for them, and re-layouts  26.8 us
    sub x2, other arithmetic, temporal_filter(): series = series - smooth_part  18.8 us
    all_to_all x1, other arithmetic, shards(): lax.all_to_all(corrected, 'date', split_axis=2, concat_axis=0, tiled=True)  13.8 us
    reshape x2, local copies, waits for them, and re-layouts, shards(): tile_view = residual.reshape(date_count, row_count, col_count // TILE, TILE)  12.3 us
    all_to_all x1, starting transfers between devices, shards(): lax.all_to_all(out_weight.reshape(devices_all, PAIR_CAP), ('date', 'strip...  10.6 us
  transfers between devices with their start and end apart: 5, of which 4 were waited for; matrix products, arithmetic and copies ran while one was open for 26% of the time, Pallas kernels for 0%

commit v1 on v0

--- a/solution.py
+++ b/solution.py
@@ -8,6 +8,22 @@
 REACH = 2
 DILATION = 8
 PAIR_CAP = 2
+
+
+def pairwise_exchange(value, axis, split, join):
+    ways, here = (lax.axis_size(axis), lax.axis_index(axis))
+    width = value.shape[split] // ways
+    shape = list(value.shape)
+    shape[split] = width
+    height = shape[join]
+    shape[join] = height * ways
+    full = jnp.zeros(shape, value.dtype)
+    for mask in range(ways):
+        part = lax.dynamic_slice_in_dim(value, (here ^ mask) * width, width, axis=split)
+        if mask:
+            part = lax.ppermute(part, axis, [(d, d ^ mask) for d in range(ways)])
+        full = lax.dynamic_update_slice_in_dim(full, part, (here ^ mask) * height, axis=join)
+    return full
 
 
 def with_halo(value, sides, width):
@@ -50,9 +66,7 @@
     across = taps_pass(padded, weights, 2, stack.shape[2])
     rimmed = with_halo(across, (("strip", 1),), RADIUS)
     corrected = stack - taps_pass(rimmed, weights, 1, stack.shape[1])
-    residual = temporal_filter(
-        lax.all_to_all(corrected, "date", split_axis=2, concat_axis=0, tiled=True), temporal_taps
-    )
+    residual = temporal_filter(pairwise_exchange(corrected, "date", 2, 0), temporal_taps)
     date_count, row_count, col_count = residual.shape
     tile_view = residual.reshape(date_count, row_count, col_count // TILE, TILE)
     picked = tile_view[:, foot_row, foot_tile, :]

time: 281 us -> 234 us (0.83)
  local copies, waits for them, and re-layouts: 62.2 us -> 33.2 us
  waiting for transfers between devices: 65.9 us -> 46.2 us
  starting transfers between devices: 32.2 us -> 43.2 us
  other arithmetic: 118 us -> 109 us
    all_to_all x1 -> x0, waiting for transfers between devices: 46.9 us -> none  [shards(): lax.all_to_all(corrected, 'date', split_axis=2, concat_axis=0, tiled=True)]
    ppermute x0 -> x7, waiting for transfers between devices: none -> 37.3 us  [pairwise_exchange(): part = lax.ppermute(part, axis, [(d, d ^ mask) for d in range(ways)])]
    unnamed x16 -> x13, local copies, waits for them, and re-layouts: 26.8 us -> 1.64 us
    all_to_all x1 -> x0, other arithmetic: 13.8 us -> none  [shards(): lax.all_to_all(corrected, 'date', split_axis=2, concat_axis=0, tiled=True)]
    ppermute x0 -> x7, starting transfers between devices: none -> 13.5 us  [pairwise_exchange(): part = lax.ppermute(part, axis, [(d, d ^ mask) for d in range(ways)])]
    sub x1 -> x0, local copies, waits for them, and re-layouts: 7.48 us -> none  [shards(): corrected = stack - taps_pass(rimmed, weights, 1, stack.shape[1])]
    all_to_all x2 -> x1, local copies, waits for them, and re-layouts: 7.29 us -> 0.51 us  [shards(): lax.all_to_all(outgoing.reshape(devices_all, PAIR_CAP, date_count), ('dat...]
    all_to_all x1 -> x0, starting transfers between devices: 6.47 us -> none  [shards(): lax.all_to_all(corrected, 'date', split_axis=2, concat_axis=0, tiled=True)]
  transfers between devices with their start and end apart: 5 -> 11, of which waited for: 4 -> 6; matrix products, arithmetic and copies ran while one was open for 26% -> 39% of each run, Pallas kernels for 0% -> 0%
where the time goes in v1:
time: 234 us; the launch traced here: 233 us
  other arithmetic  109 us (47%)
  waiting for transfers between devices  46.2 us (20%)
  starting transfers between devices  43.2 us (18%)
  local copies, waits for them, and re-layouts  33.2 us (14%)
    add x1, other arithmetic, taps_pass(): summed + weights[k] * lax.slice_in_dim(padded, k, k + length, axis=axis_num)  41.7 us
    sub x1, other arithmetic, shards(): corrected = stack - taps_pass(rimmed, weights, 1, stack.shape[1])  38.7 us
    ppermute x7, waiting for transfers between devices, pairwise_exchange(): part = lax.ppermute(part, axis, [(d, d ^ mask) for d in range(ways)])  37.3 us
    sub x2, other arithmetic, temporal_filter(): series = series - smooth_part  18.7 us
    ppermute x7, starting transfers between devices, pairwise_exchange(): part = lax.ppermute(part, axis, [(d, d ^ mask) for d in range(ways)])  13.5 us
    all_to_all x1, starting transfers between devices, shards(): lax.all_to_all(outgoing.reshape(devices_all, PAIR_CAP, date_count), ('dat...  12.4 us
    reshape x2, local copies, waits for them, and re-layouts, shards(): tile_view = residual.reshape(date_count, row_count, col_count // TILE, TILE)  12.3 us
    all_to_all x1, starting transfers between devices, shards(): lax.all_to_all(out_weight.reshape(devices_all, PAIR_CAP), ('date', 'strip...  12.1 us
  transfers between devices with their start and end apart: 11, of which 6 were waited for; matrix products, arithmetic and copies ran while one was open for 39% of the time, Pallas kernels for 0%

profile of v1, /device:TPU:1, one launch (start us, length us, event | category | flops | bytes accessed | tf_op | source)
XLA Modules:
  0.0 233.3 jit_solution(5026497901514885920)
XLA Ops:
  0.6 1.3 reduce_sum.47
  1.9 1.3 broadcast_divide_fusion.1
  3.2 0.7 fusion.75
  3.9 0.0 copy-start.1
  3.9 41.7 %multiply_add_fusion = f32[8,64,2048]{2,1,0:T(8,128)} fusion(f32[8,64,2048]{2,1,0:T(8,128)} %param.7, f32[]{:T(128)} %bitcast.12, f32[]{:T(128)} %bitcast.11, f32[]{:T(128)} %bitcast.10, f32[]{:T(128)} %bitcast.9, f32[]{:T(128)} %bitcast.8, f32[]{:T(128)} %bitcast.7, f32[]{:T(128)} %bitcast.6, f32[]{:T(128)} %bitcast.5, f32[]{:T(128)} %bitcast.4, ...), kind=kLoop, calls=%fused_computation.79 | loop fusion | flops 26214400 | bytes 8388660 | tf_op jit(solution)/shard_map/add | solution.py:45
  45.7 1.3 fusion.73
  46.9 4.0 %collective-permute-start = (f32[8,6,2048]{2,1,0:T(8,128)S(1)}, f32[8,6,2048]{2,1,0:T(8,128)S(1)}, u32[]{:S(2)}, u32[]{:S(2)}) collective-permute-start(f32[8,6,2048]{2,1,0:T(8,128)S(1)} %get-tuple-element.23), channel_id=1, source_target_pairs={{0,1},{1,2},{2,3},{3,4},{4,5},{5,6},{6,7},{7,8},{8,9},{9,10},{10,1... | collective-permute-start | bytes 1179656 | tf_op jit(solution)/shard_map/ppermute | solution.py:36
  50.9 1.3 collective-permute-start.1
  52.2 0.0 copy-done.2
  52.2 0.2 convert_reduce_fusion
  52.4 0.0 copy-done.1
  52.4 0.2 fusion.58
  52.6 0.8 all_to_all.11
  53.4 12.1 %all-to-all-start = ((f32[128,1,2]{2,1,0:T(1,128)}), f32[128,1,2]{2,1,0:T(1,128)S(1)}, u32[]{:S(2)}, u32[]{:S(2)}) async-start(f32[128,1,2]{2,1,0:T(1,128)} %bitcast.28), calls=%async_computation | async-start | bytes 131072 | tf_op jit(solution)/shard_map/all_to_all | solution.py:97
  65.6 0.0 collective-permute-done
  65.6 0.0 collective-permute-done.1
  65.6 38.7 %fusion.4 = f32[8,64,2048]{2,1,0:T(8,128)S(1)} fusion(f32[8,64,2048]{2,1,0:T(8,128)} %param.7, f32[8,64,2048]{2,1,0:T(8,128)} %multiply_add_fusion, f32[8,6,2048]{2,1,0:T(8,128)S(1)} %collective-permute-done.1, f32[8,6,2048]{2,1,0:T(8,128)S(1)} %collective-permute-done, f32[]{:T(128)} %bitcast.12, f32[]{:T(128)} %bitcast.11, f32[]{:T(128)} %bitcast.10, ...), kind=kLoop, calls=%fused_computation.29 | loop fusion | flops 39845888 | bytes 13369396 | tf_op jit(solution)/shard_map/sub | solution.py:68
  104.3 2.5 %broadcast_in_dim.14 = f32[64,64,256]{2,1,0:T(8,128)} broadcast(f32[]{:T(128)} %constant.15.clone.1), dimensions={} | broadcast | bytes 4194308 | tf_op jit(solution)/shard_map/broadcast_in_dim | solution.py:20
  106.9 1.9 constant_dynamic-slice_fusion
  108.7 1.6 collective-permute-start.2
  110.3 1.3 collective-permute-start.3
  111.6 0.1 fusion.63
  111.7 0.4 collective-permute-start.4
  112.1 2.9 %collective-permute-start.5 = (f32[8,64,256]{2,1,0:T(8,128)}, f32[8,64,256]{2,1,0:T(8,128)S(1)}, u32[]{:S(2)}, u32[]{:S(2)}) collective-permute-start(f32[8,64,256]{2,1,0:T(8,128)} %get-tuple-element.18), channel_id=1, source_target_pairs={{0,64},{16,80},{32,96},{48,112},{64,0},{80,16},{96,32},{112,48},{1... | collective-permute-start | bytes 1572872 | tf_op jit(solution)/shard_map/ppermute | solution.py:24
  115.0 0.0 copy-done.3
  115.0 0.0 copy-done.4
  115.1 0.7 collective-permute-start.6
  115.8 0.7 fusion.74
  116.5 0.0 collective-permute-done.2
  116.5 2.8 %collective-permute-start.7 = (f32[8,64,256]{2,1,0:T(8,128)}, f32[8,64,256]{2,1,0:T(8,128)S(1)}, u32[]{:S(2)}, u32[]{:S(2)}) collective-permute-start(f32[8,64,256]{2,1,0:T(8,128)} %get-tuple-element.16), channel_id=1, source_target_pairs={{0,96},{16,112},{32,64},{48,80},{64,32},{80,48},{96,0},{112,16},{1... | collective-permute-start | bytes 1572872 | tf_op jit(solution)/shard_map/ppermute | solution.py:24
  119.3 0.8 constant_dynamic-update-slice_fusion.6
  120.1 3.9 %collective-permute-done.3 = f32[8,64,256]{2,1,0:T(8,128)S(1)} collective-permute-done((f32[8,64,256]{2,1,0:T(8,128)}, f32[8,64,256]{2,1,0:T(8,128)S(1)}, u32[]{:S(2)}, u32[]{:S(2)}) %collective-permute-start.3) | collective-permute-done | bytes 524320 | tf_op jit(solution)/shard_map/ppermute | solution.py:24
  124.1 3.8 %collective-permute-start.8 = (f32[8,64,256]{2,1,0:T(8,128)S(1)}, f32[8,64,256]{2,1,0:T(8,128)S(1)}, u32[]{:S(2)}, u32[]{:S(2)}) collective-permute-start(f32[8,64,256]{2,1,0:T(8,128)S(1)} %get-tuple-element.15), channel_id=1, source_target_pairs={{0,112},{16,96},{32,80},{48,64},{64,48},{80,32},{96,16},{112,0},{1... | collective-permute-start | bytes 1572872 | tf_op jit(solution)/shard_map/ppermute | solution.py:24
  127.9 0.8 constant_dynamic-update-slice_fusion.5
  128.7 7.4 %collective-permute-done.4 = f32[8,64,256]{2,1,0:T(8,128)S(1)} collective-permute-done((f32[8,64,256]{2,1,0:T(8,128)}, f32[8,64,256]{2,1,0:T(8,128)S(1)}, u32[]{:S(2)}, u32[]{:S(2)}) %collective-permute-start.4) | collective-permute-done | bytes 524320 | tf_op jit(solution)/shard_map/ppermute | solution.py:24
  136.1 0.8 constant_dynamic-update-slice_fusion.4
  136.9 12.1 %collective-permute-done.5 = f32[8,64,256]{2,1,0:T(8,128)S(1)} collective-permute-done((f32[8,64,256]{2,1,0:T(8,128)}, f32[8,64,256]{2,1,0:T(8,128)S(1)}, u32[]{:S(2)}, u32[]{:S(2)}) %collective-permute-start.5) | collective-permute-done | bytes 524320 | tf_op jit(solution)/shard_map/ppermute | solution.py:24
  149.0 0.8 constant_dynamic-update-slice_fusion.3
  149.9 10.5 %collective-permute-done.6 = f32[8,64,256]{2,1,0:T(8,128)S(1)} collective-permute-done((f32[8,64,256]{2,1,0:T(8,128)}, f32[8,64,256]{2,1,0:T(8,128)S(1)}, u32[]{:S(2)}, u32[]{:S(2)}) %collective-permute-start.6) | collective-permute-done | bytes 524320 | tf_op jit(solution)/shard_map/ppermute | solution.py:24
  160.4 0.8 constant_dynamic-update-slice_fusion.2
  161.3 0.0 collective-permute-done.7
  161.3 0.8 constant_dynamic-update-slice_fusion.1
  162.1 3.3 %collective-permute-done.8 = f32[8,64,256]{2,1,0:T(8,128)S(1)} collective-permute-done((f32[8,64,256]{2,1,0:T(8,128)S(1)}, f32[8,64,256]{2,1,0:T(8,128)S(1)}, u32[]{:S(2)}, u32[]{:S(2)}) %collective-permute-start.8) | collective-permute-done | bytes 524320 | tf_op jit(solution)/shard_map/ppermute | solution.py:24
  165.4 0.8 constant_dynamic-update-slice_fusion
  166.2 12.0 %add_subtract_fusion = f32[64,64,256]{2,1,0:T(8,128)S(1)} fusion(f32[64,64,256]{2,1,0:T(8,128)} %constant_dynamic-update-slice_fusion, f32[]{:T(128)} %bitcast.17, f32[]{:T(128)} %bitcast.16, f32[]{:T(128)} %bitcast.15, f32[]{:T(128)} %bitcast.14, f32[]{:T(128)} %bitcast.13), kind=kLoop, calls=%fused_computation.72 | loop fusion | flops 10485760 | bytes 8388628 | tf_op jit(solution)/shard_map/sub | solution.py:59
  178.2 6.7 %fusion.38 = f32[64,64,256]{2,1,0:T(8,128)} fusion(f32[64,64,256]{2,1,0:T(8,128)S(1)} %add_subtract_fusion, f32[]{:T(128)} %bitcast.22, f32[]{:T(128)} %bitcast.21, f32[]{:T(128)} %bitcast.20, f32[]{:T(128)} %bitcast.19, f32[]{:T(128)} %bitcast.18), kind=kLoop, calls=%fused_computation.63 | loop fusion | flops 10485760 | bytes 8388628 | tf_op jit(solution)/shard_map/sub | solution.py:59
  185.0 5.8 %reshape.61 = f32[64,64,2,128]{3,2,1,0:T(2,128)} reshape(f32[64,64,256]{2,1,0:T(8,128)} %fusion.38) | data formatting | bytes 8388608 | tf_op jit(solution)/shard_map/reshape | solution.py:71
  190.7 6.6 %copy.20 = f32[64,64,2,128]{3,0,2,1:T(8,128)} copy(f32[64,64,2,128]{3,2,1,0:T(2,128)} %reshape.61) | data formatting | bytes 8388608 | tf_op jit(solution)/shard_map/reshape | solution.py:71
  197.3 5.0 %gather_fusion = f32[128,64,128]{2,1,0:T(8,128)} fusion(f32[64,64,2,128]{3,0,2,1:T(8,128)} %copy.20, s32[128]{0:T(128)S(1)} %fusion.67), kind=kCustom, calls=%fused_computation | custom fusion | bytes 8389632 | tf_op jit(solution)/shard_map/gather | solution.py:72
  202.3 3.4 %multiply_reduce_fusion = f32[128,64]{1,0:T(8,128)S(1)} fusion(f32[128,64,128]{2,1,0:T(8,128)} %gather_fusion, f32[128,128]{1,0:T(8,128)S(1)} %fusion.63), kind=kLoop, calls=%fused_computation.71 | loop fusion | flops 2088960 | bytes 4292608 | tf_op jit(solution)/shard_map/reduce_sum | solution.py:75
  205.7 0.4 fusion.57
  206.0 0.8 reshape.84
  206.8 0.0 all-to-all-done
  206.8 12.4 %all-to-all-start.1 = ((f32[128,1,128]{2,1,0:T(1,128)}), f32[128,1,128]{2,1,0:T(1,128)S(1)}, u32[]{:S(2)}, u32[]{:S(2)}) async-start(f32[128,1,128]{2,1,0:T(1,128)} %reshape.84), calls=%async_computation.1 | async-start | bytes 131072 | tf_op jit(solution)/shard_map/all_to_all | solution.py:90
  219.2 0.7 reduce_sum.52
  220.0 8.9 %all-to-all-done.1 = f32[128,1,128]{2,1,0:T(1,128)S(1)} async-done(((f32[128,1,128]{2,1,0:T(1,128)}), f32[128,1,128]{2,1,0:T(1,128)S(1)}, u32[]{:S(2)}, u32[]{:S(2)}) %all-to-all-start.1) | async-done | bytes 65568 | tf_op jit(solution)/shard_map/all_to_all | solution.py:90
  228.9 0.5 broadcast.84
  229.4 0.8 reduce.3
  230.2 0.1 reshape.85
  230.4 0.2 multiply_reduce_fusion.1
  230.6 0.6 broadcast_divide_fusion
  231.2 1.1 fusion.76
  232.4 0.2 subtract_select_fusion
  232.6 0.7 copy.22
  (9 shorter events, 0.0 us)
Async XLA Ops:
  3.9 48.3 %copy-start.2 = (s32[128,1]{0,1:T(1,128)S(1)}, s32[128,1]{0,1:T(1,128)}, u32[]{:S(2)}) copy-start(s32[128,1]{0,1:T(1,128)} %param.13) | copy-start | bytes 1540
  3.9 48.5 %copy-start.1 = (s32[128]{0:T(128)S(1)}, s32[128]{0:T(128)}, u32[]{:S(2)}) copy-start(s32[128]{0:T(128)} %param.12) | copy-start | bytes 1540
  46.9 18.6 %collective-permute-start = (f32[8,6,2048]{2,1,0:T(8,128)S(1)}, f32[8,6,2048]{2,1,0:T(8,128)S(1)}, u32[]{:S(2)}, u32[]{:S(2)}) collective-permute-start(f32[8,6,2048]{2,1,0:T(8,128)S(1)} %get-tuple-element.23), channel_id=1, source_target_pairs={{0,1},{1,2},{2,3},{3,4},{4,5},{5,6},{6,7},{7,8},{8,9},{9,10},{10,1... | collective-permute-start | bytes 1179656 | tf_op jit(solution)/shard_map/ppermute | solution.py:36
  50.9 14.6 %collective-permute-start.1 = (f32[8,6,2048]{2,1,0:T(8,128)S(1)}, f32[8,6,2048]{2,1,0:T(8,128)S(1)}, u32[]{:S(2)}, u32[]{:S(2)}) collective-permute-start(f32[8,6,2048]{2,1,0:T(8,128)S(1)} %get-tuple-element.24), channel_id=1, source_target_pairs={{1,0},{2,1},{3,2},{4,3},{5,4},{6,5},{7,6},{8,7},{9,8},{10,9},{11,1... | collective-permute-start | bytes 1179656 | tf_op jit(solution)/shard_map/ppermute | solution.py:37
  53.4 153.4 %all-to-all-start = ((f32[128,1,2]{2,1,0:T(1,128)}), f32[128,1,2]{2,1,0:T(1,128)S(1)}, u32[]{:S(2)}, u32[]{:S(2)}) async-start(f32[128,1,2]{2,1,0:T(1,128)} %bitcast.28), calls=%async_computation | async-start | bytes 131072 | tf_op jit(solution)/shard_map/all_to_all | solution.py:97
  106.9 8.2 %copy-start.3 = (s32[128]{0:T(128)S(1)}, s32[128]{0:T(128)}, u32[]{:S(2)}) copy-start(s32[128]{0:T(128)} %param.11) | copy-start | bytes 1540
  106.9 8.2 %copy-start.4 = (s32[128]{0:T(128)S(1)}, s32[128]{0:T(128)}, u32[]{:S(2)}) copy-start(s32[128]{0:T(128)} %param.10) | copy-start | bytes 1540
  106.9 8.9 %copy-start = (f32[2,5]{1,0:T(2,128)S(1)}, f32[2,5]{1,0:T(2,128)}, u32[]{:S(2)}) copy-start(f32[2,5]{1,0:T(2,128)} %param.9) | copy-start | bytes 124
  108.7 7.7 %collective-permute-start.2 = (f32[8,64,256]{2,1,0:T(8,128)}, f32[8,64,256]{2,1,0:T(8,128)S(1)}, u32[]{:S(2)}, u32[]{:S(2)}) collective-permute-start(f32[8,64,256]{2,1,0:T(8,128)} %get-tuple-element.21), channel_id=1, source_target_pairs={{0,16},{16,0},{32,48},{48,32},{64,80},{80,64},{96,112},{112,96},{1... | collective-permute-start | bytes 1572872 | tf_op jit(solution)/shard_map/ppermute | solution.py:24
  110.3 13.8 %collective-permute-start.3 = (f32[8,64,256]{2,1,0:T(8,128)}, f32[8,64,256]{2,1,0:T(8,128)S(1)}, u32[]{:S(2)}, u32[]{:S(2)}) collective-permute-start(f32[8,64,256]{2,1,0:T(8,128)} %get-tuple-element.20), channel_id=1, source_target_pairs={{0,32},{16,48},{32,0},{48,16},{64,96},{80,112},{96,64},{112,80},{1... | collective-permute-start | bytes 1572872 | tf_op jit(solution)/shard_map/ppermute | solution.py:24
  111.7 24.4 %collective-permute-start.4 = (f32[8,64,256]{2,1,0:T(8,128)}, f32[8,64,256]{2,1,0:T(8,128)S(1)}, u32[]{:S(2)}, u32[]{:S(2)}) collective-permute-start(f32[8,64,256]{2,1,0:T(8,128)} %get-tuple-element.19), channel_id=1, source_target_pairs={{0,48},{16,32},{32,16},{48,0},{64,112},{80,96},{96,80},{112,64},{1... | collective-permute-start | bytes 1572872 | tf_op jit(solution)/shard_map/ppermute | solution.py:24
  112.1 36.9 %collective-permute-start.5 = (f32[8,64,256]{2,1,0:T(8,128)}, f32[8,64,256]{2,1,0:T(8,128)S(1)}, u32[]{:S(2)}, u32[]{:S(2)}) collective-permute-start(f32[8,64,256]{2,1,0:T(8,128)} %get-tuple-element.18), channel_id=1, source_target_pairs={{0,64},{16,80},{32,96},{48,112},{64,0},{80,16},{96,32},{112,48},{1... | collective-permute-start | bytes 1572872 | tf_op jit(solution)/shard_map/ppermute | solution.py:24
  115.1 45.4 %collective-permute-start.6 = (f32[8,64,256]{2,1,0:T(8,128)}, f32[8,64,256]{2,1,0:T(8,128)S(1)}, u32[]{:S(2)}, u32[]{:S(2)}) collective-permute-start(f32[8,64,256]{2,1,0:T(8,128)} %get-tuple-element.17), channel_id=1, source_target_pairs={{0,80},{16,64},{32,112},{48,96},{64,16},{80,0},{96,48},{112,32},{1... | collective-permute-start | bytes 1572872 | tf_op jit(solution)/shard_map/ppermute | solution.py:24
  116.5 44.8 %collective-permute-start.7 = (f32[8,64,256]{2,1,0:T(8,128)}, f32[8,64,256]{2,1,0:T(8,128)S(1)}, u32[]{:S(2)}, u32[]{:S(2)}) collective-permute-start(f32[8,64,256]{2,1,0:T(8,128)} %get-tuple-element.16), channel_id=1, source_target_pairs={{0,96},{16,112},{32,64},{48,80},{64,32},{80,48},{96,0},{112,16},{1... | collective-permute-start | bytes 1572872 | tf_op jit(solution)/shard_map/ppermute | solution.py:24
  124.1 41.3 %collective-permute-start.8 = (f32[8,64,256]{2,1,0:T(8,128)S(1)}, f32[8,64,256]{2,1,0:T(8,128)S(1)}, u32[]{:S(2)}, u32[]{:S(2)}) collective-permute-start(f32[8,64,256]{2,1,0:T(8,128)S(1)} %get-tuple-element.15), channel_id=1, source_target_pairs={{0,112},{16,96},{32,80},{48,64},{64,48},{80,32},{96,16},{112,0},{1... | collective-permute-start | bytes 1572872 | tf_op jit(solution)/shard_map/ppermute | solution.py:24
  206.8 22.1 %all-to-all-start.1 = ((f32[128,1,128]{2,1,0:T(1,128)}), f32[128,1,128]{2,1,0:T(1,128)S(1)}, u32[]{:S(2)}, u32[]{:S(2)}) async-start(f32[128,1,128]{2,1,0:T(1,128)} %reshape.84), calls=%async_computation.1 | async-start | bytes 131072 | tf_op jit(solution)/shard_map/all_to_all | solution.py:90
